TPU v7x, 32 devices: a whole 2x2x4 slice. The times are simulated.
32 devices in a mesh: row: 8 (over y, x, core), col: 4 (over z).
Axes of the slice: x: 2, y: 2, z: 4, core: 2. Of those that a mesh axis runs over, the one named last changes fastest.
Arguments:
- covariance: float32 [2, 8192, 8192], P(None, 'row', 'col'), as said below
- forcing: float32 [2, 8192, 8192], P(None, 'row', 'col'), as said below
- coupling: float32 [2, 64, 64], replicated, may hold values from -0.5 to 0.5
- vertical: float32 [2, 128, 128], replicated, may hold values from -0.375 to 0.375
- damping: float32 [64, 128], replicated, may hold values from 0.3 to 3
- advection: float32 [64, 128], replicated, may hold values from -2 to 2
Outputs:
- advanced: float32 [2, 8192, 8192], P(None, 'row', 'col')
Inputs may be any that keep to these rules, and one draw needn't show every extreme that they name: The covariance equals its conjugate transpose: the real plane is symmetric, the imaginary plane antisymmetric. The forcing equals its conjugate transpose: the real plane is symmetric, the imaginary plane antisymmetric.
All inputs are finite; a program needn't handle non-finite values.
Results may differ from a plain program's by a relative error of at most 0.000073.
Values sent between devices are 32-bit elements; how exact they have to be, the bound alone decides.
A program may use at most 320 MiB of HBM per device.

v0:
```python
import jax
import jax.numpy as jnp
from jax import lax
from jax.sharding import PartitionSpec as P

step_size = 0.25


def complex_einsum(pattern, factor, values):

    def single(factor_part, value_part):
        return jnp.einsum(pattern, factor_part, value_part, precision=lax.Precision.HIGHEST)

    real_part = single(factor[0], values[0]) - single(factor[1], values[1])
    imag_part = single(factor[0], values[1]) + single(factor[1], values[0])
    return jnp.stack([real_part, imag_part])


def complex_scale(factor, values):
    real_part = factor[0] * values[0] - factor[1] * values[1]
    imag_part = factor[0] * values[1] + factor[1] * values[0]
    return jnp.stack([real_part, imag_part])


def conjugate(values):
    return jnp.stack([values[0], -values[1]])


def left_apply(by_rows, coupling, vertical, rates):
    total = complex_einsum("lm,amj->alj", vertical, by_rows)
    total = total + complex_einsum("ab,blj->alj", coupling, by_rows)
    return total + complex_scale(rates[:, :, :, None], by_rows)


def right_apply(by_cols, coupling, vertical, rates):
    total = complex_einsum("lm,iam->ial", conjugate(vertical), by_cols)
    total = total + complex_einsum("ab,ibl->ial", conjugate(coupling), by_cols)
    return total + complex_scale(conjugate(rates)[:, None], by_cols)


def tendency(block_tile, forcing, coupling, vertical, rates):
    rows_here = block_tile.shape[1]
    cols_here = block_tile.shape[2]
    levels = vertical.shape[1]
    lats_row = rows_here // levels
    lats_col = cols_here // levels
    by_rows = block_tile.reshape(2, lats_row, levels, cols_here)
    regrouped = lax.all_to_all(by_rows, "row", split_axis=3, concat_axis=1, tiled=True)
    applied = left_apply(regrouped, coupling, vertical, rates)
    left_term = lax.all_to_all(applied, "row", split_axis=1, concat_axis=3, tiled=True)
    left_term = left_term.reshape(2, rows_here, cols_here)
    by_cols = block_tile.reshape(2, rows_here, lats_col, levels)
    regrouped_cols = lax.all_to_all(by_cols, "col", split_axis=1, concat_axis=2, tiled=True)
    applied_cols = right_apply(regrouped_cols, coupling, vertical, rates)
    right_term = lax.all_to_all(
        applied_cols, "col", split_axis=2, concat_axis=1, tiled=True
    ).reshape(2, rows_here, cols_here)
    return left_term + right_term + forcing


def shards(covariance, forcing, coupling, vertical, damping, advection):
    rates = jnp.stack([-damping, advection])
    first_rate = tendency(covariance, forcing, coupling, vertical, rates)
    midpoint = covariance + 0.5 * step_size * first_rate
    return covariance + step_size * tendency(midpoint, forcing, coupling, vertical, rates)


def solution(mesh):
    return jax.shard_map(
        shards,
        mesh=mesh,
        in_specs=(P(None, "row", "col"), P(None, "row", "col"), P(), P(), P(), P()),
        out_specs=P(None, "row", "col"),
        check_vma=False,
    )
```

profile of v0, /device:TPU:0, one launch (start us, length us, event | category | flops | bytes accessed | tf_op | source)
XLA Modules:
  0.0 2441.1 jit_solution(17442187832632348149)
XLA Ops:
  0.0 17.6 copy.149
  39.9 168.1 %all-to-all-done = f32[2,8,128,2048]{2,1,0,3:T(8,128)} async-done(((f32[2,8,128,2048]{2,1,0,3:T(8,128)}), f32[2,8,128,2048]{2,1,0,3:T(8,128)}, u32[]{:S(2)}, u32[]{:S(2)}) %all-to-all-start) | async-done | bytes 16777248 | tf_op jit(solution)/shard_map/all_to_all | solution.py:48
  397.3 19.0 add_bitcast_fusion.4
  439.1 137.1 %all-to-all-done.2 = f32[2,1024,16,128]{3,2,0,1:T(8,128)} async-done(((f32[2,1024,16,128]{3,2,0,1:T(8,128)}), f32[2,1024,16,128]{3,2,0,1:T(8,128)}, u32[]{:S(2)}, u32[]{:S(2)}) %all-to-all-start.2) | async-done | bytes 16777248 | tf_op jit(solution)/shard_map/all_to_all | solution.py:53
  641.2 17.4 fusion.20
  720.1 41.0 %fusion.6 = (f32[1,256,64,128]{3,1,2,0:T(8,128)}, f32[1,256,64,128]{3,1,2,0:T(8,128)}) fusion(f32[256,128,64]{1,2,0:T(8,128)} %fusion.20, f32[256,128,64]{1,2,0:T(8,128)} %fusion.16, f32[256,128,64]{1,2,0:T(8,128)} %fusion.18, f32[256,128,64]{1,2,0:T(8,128)} %fusion.22), kind=kLoop, calls=%fused_computation.16 | loop fusion | flops 4194304 | bytes 50331648 | tf_op jit(solution)/shard_map/stack | solution.py:16
  791.0 17.4 copy.164
  808.4 18.0 reshape.251
  826.3 328.4 %all-to-all-done.3 = f32[2,256,64,128]{3,1,0,2:T(8,128)} async-done(((f32[2,256,64,128]{3,1,0,2:T(8,128)}), f32[2,256,64,128]{3,1,0,2:T(8,128)}, u32[]{:S(2)}, u32[]{:S(2)}) %all-to-all-start.3) | async-done | bytes 16777248 | tf_op jit(solution)/shard_map/all_to_all | solution.py:55
  1154.7 17.8 copy.249
  1172.5 18.0 reshape.253
  1190.4 29.2 %multiply_add_fusion.1 = f32[2,1024,2048]{2,1,0:T(8,128)} fusion(f32[2,1024,2048]{2,1,0:T(8,128)} %param.6, f32[2,1024,2048]{2,1,0:T(8,128)} %param.7, f32[2,1024,2048]{2,1,0:T(8,128)} %reshape.251, f32[2,1024,2048]{2,1,0:T(8,128)} %reshape.253), kind=kLoop, calls=%fused_computation.10 | loop fusion | flops 16777216 | bytes 83886080 | tf_op jit(solution)/shard_map/add | solution.py:64
  1219.6 17.7 copy.181
  1259.5 167.4 %all-to-all-done.4 = f32[2,8,128,2048]{2,1,0,3:T(8,128)} async-done(((f32[2,8,128,2048]{2,1,0,3:T(8,128)}), f32[2,8,128,2048]{2,1,0,3:T(8,128)}, u32[]{:S(2)}, u32[]{:S(2)}) %all-to-all-start.4) | async-done | bytes 16777248 | tf_op jit(solution)/shard_map/all_to_all | solution.py:48
  1659.0 135.3 %all-to-all-done.6 = f32[2,1024,16,128]{3,2,0,1:T(8,128)} async-done(((f32[2,1024,16,128]{3,2,0,1:T(8,128)}), f32[2,1024,16,128]{3,2,0,1:T(8,128)}, u32[]{:S(2)}, u32[]{:S(2)}) %all-to-all-start.6) | async-done | bytes 16777248 | tf_op jit(solution)/shard_map/all_to_all | solution.py:53
  1845.3 17.4 fusion.12
  1934.3 18.2 fusion.5
  1952.6 18.4 fusion.4
  2012.2 17.4 copy.196
  2029.6 18.0 reshape.255
  2047.5 328.4 %all-to-all-done.7 = f32[2,256,64,128]{3,1,0,2:T(8,128)} async-done(((f32[2,256,64,128]{3,1,0,2:T(8,128)}), f32[2,256,64,128]{3,1,0,2:T(8,128)}, u32[]{:S(2)}, u32[]{:S(2)}) %all-to-all-start.7) | async-done | bytes 16777248 | tf_op jit(solution)/shard_map/all_to_all | solution.py:55
  2375.9 17.8 copy.212
  2393.7 18.0 reshape.257
  2411.7 29.2 %multiply_add_fusion = f32[2,1024,2048]{2,1,0:T(8,128)} fusion(f32[2,1024,2048]{2,1,0:T(8,128)} %param.6, f32[2,1024,2048]{2,1,0:T(8,128)} %param.7, f32[2,1024,2048]{2,1,0:T(8,128)} %reshape.255, f32[2,1024,2048]{2,1,0:T(8,128)} %reshape.257), kind=kLoop, calls=%fused_computation.9 | loop fusion | flops 16777216 | bytes 83886080 | tf_op jit(solution)/shard_map/add | solution.py:65
  (136 shorter events, 808.5 us)
Async XLA Ops:
  17.6 190.4 %all-to-all-start = ((f32[2,8,128,2048]{2,1,0,3:T(8,128)}), f32[2,8,128,2048]{2,1,0,3:T(8,128)}, u32[]{:S(2)}, u32[]{:S(2)}) async-start(f32[2,8,128,2048]{2,1,0,3:T(8,128)} %copy.149), calls=%async_computation | async-start | bytes 33554432 | tf_op jit(solution)/shard_map/all_to_all | solution.py:48
  39.9 175.3 %copy-start.13 = (f32[64,128]{1,0:T(8,128)S(1)}, f32[64,128]{1,0:T(8,128)}, u32[]{:S(2)}) copy-start(f32[64,128]{1,0:T(8,128)} %param.10) | copy-start | bytes 98308
  208.0 368.2 %all-to-all-start.2 = ((f32[2,1024,16,128]{3,2,0,1:T(8,128)}), f32[2,1024,16,128]{3,2,0,1:T(8,128)}, u32[]{:S(2)}, u32[]{:S(2)}) async-start(f32[2,1024,16,128]{3,2,0,1:T(8,128)} %copy.213), calls=%async_computation.2 | async-start | bytes 33554432 | tf_op jit(solution)/shard_map/all_to_all | solution.py:53
  215.2 497.9 %copy-start.7 = (f32[64,128]{1,0:T(8,128)}, f32[64,128]{1,0:T(8,128)S(1)}, u32[]{:S(2)}) copy-start(f32[64,128]{1,0:T(8,128)S(1)} %neg.27) | copy-start | bytes 98308
  349.3 20.4 slice-start.6
  349.3 31.2 %slice-start.4 = ((s8[8388608]{0:T(1024)(128)(4,1)}), s8[4194304]{0:T(1024)(128)(4,1)S(1)}, s32[]{:S(2)}) async-start(s8[8388608]{0:T(1024)(128)(4,1)} %bitcast.244), calls=%async_computation.12 | async-start | bytes 8388608
  360.4 20.2 slice-start.5
  380.6 9.6 copy-start.9
  576.2 207.7 %all-to-all-start.1 = ((f32[2,64,128,256]{2,3,0,1:T(8,128)}), f32[2,64,128,256]{2,3,0,1:T(8,128)}, u32[]{:S(2)}, u32[]{:S(2)}) async-start(f32[2,64,128,256]{2,3,0,1:T(8,128)} %copy.163), calls=%async_computation.1 | async-start | bytes 33554432 | tf_op jit(solution)/shard_map/all_to_all | solution.py:50
  582.2 130.9 %copy-start.11 = (f32[64,128]{1,0:T(8,128)}, f32[64,128]{1,0:T(8,128)S(1)}, u32[]{:S(2)}) copy-start(f32[64,128]{1,0:T(8,128)S(1)} %neg.32) | copy-start | bytes 98308
  784.0 370.8 %all-to-all-start.3 = ((f32[2,256,64,128]{3,1,0,2:T(8,128)}), f32[2,256,64,128]{3,1,0,2:T(8,128)}, u32[]{:S(2)}, u32[]{:S(2)}) async-start(f32[2,256,64,128]{3,1,0,2:T(8,128)} %copy.179), calls=%async_computation.3 | async-start | bytes 33554432 | tf_op jit(solution)/shard_map/all_to_all | solution.py:55
  1237.3 189.7 %all-to-all-start.4 = ((f32[2,8,128,2048]{2,1,0,3:T(8,128)}), f32[2,8,128,2048]{2,1,0,3:T(8,128)}, u32[]{:S(2)}, u32[]{:S(2)}) async-start(f32[2,8,128,2048]{2,1,0,3:T(8,128)} %copy.181), calls=%async_computation.4 | async-start | bytes 33554432 | tf_op jit(solution)/shard_map/all_to_all | solution.py:48
  1426.9 367.4 %all-to-all-start.6 = ((f32[2,1024,16,128]{3,2,0,1:T(8,128)}), f32[2,1024,16,128]{3,2,0,1:T(8,128)}, u32[]{:S(2)}, u32[]{:S(2)}) async-start(f32[2,1024,16,128]{3,2,0,1:T(8,128)} %copy.197), calls=%async_computation.6 | async-start | bytes 33554432 | tf_op jit(solution)/shard_map/all_to_all | solution.py:53
  1565.3 18.7 slice-start.2
  1565.3 27.8 %slice-start = ((s8[8388608]{0:T(1024)(128)(4,1)}), s8[4194304]{0:T(1024)(128)(4,1)S(1)}, s32[]{:S(2)}) async-start(s8[8388608]{0:T(1024)(128)(4,1)} %bitcast.233), calls=%async_computation.8 | async-start | bytes 8388608
  1574.7 9.4 slice-start.3
  1574.7 18.5 slice-start.1
  1613.6 11.3 copy-start.8
  1613.6 11.3 copy-start.10
  1794.3 210.6 %all-to-all-start.5 = ((f32[2,64,128,256]{2,3,0,1:T(8,128)}), f32[2,64,128,256]{2,3,0,1:T(8,128)}, u32[]{:S(2)}, u32[]{:S(2)}) async-start(f32[2,64,128,256]{2,3,0,1:T(8,128)} %copy.195), calls=%async_computation.5 | async-start | bytes 33554432 | tf_op jit(solution)/shard_map/all_to_all | solution.py:50
  1819.1 106.0 %copy-start = (f32[1,256,4,16,128]{4,1,3,2,0:T(8,128)}, f32[1,256,4,16,128]{4,1,3,2,0:T(8,128)S(1)}, u32[]{:S(2)}) copy-start(f32[1,256,4,16,128]{4,1,3,2,0:T(8,128)S(1)} %copy.199) | copy-start | bytes 25165828
  1828.1 86.1 %copy-start.1 = (f32[1,256,4,16,128]{4,1,3,2,0:T(8,128)}, f32[1,256,4,16,128]{4,1,3,2,0:T(8,128)S(1)}, u32[]{:S(2)}) copy-start(f32[1,256,4,16,128]{4,1,3,2,0:T(8,128)S(1)} %copy.200) | copy-start | bytes 25165828
  1952.6 18.4 copy-start.12
  2004.9 371.0 %all-to-all-start.7 = ((f32[2,256,64,128]{3,1,0,2:T(8,128)}), f32[2,256,64,128]{3,1,0,2:T(8,128)}, u32[]{:S(2)}, u32[]{:S(2)}) async-start(f32[2,256,64,128]{3,1,0,2:T(8,128)} %copy.211), calls=%async_computation.7 | async-start | bytes 33554432 | tf_op jit(solution)/shard_map/all_to_all | solution.py:55
  (6 other events, 54.1 us)
where the time goes:
time: 2450 us; the launch traced here: 2440 us
  waiting for transfers between devices  1260 us (51%)
  local copies, waits for them, and re-layouts  457 us (19%)
  matrix products  386 us (16%)
  other arithmetic  281 us (11%)
  starting transfers between devices  52 us (2%)
    all_to_all x2, waiting for transfers between devices, tendency(): lax.all_to_all(applied_cols, 'col', split_axis=2, concat_axis=1, tiled=True)  657 us
    dot_general x32, matrix products, single(): jnp.einsum(pattern, factor_part, value_part, precision=lax.Precision.HIGH...  386 us
    all_to_all x2, waiting for transfers between devices, tendency(): lax.all_to_all(by_rows, 'row', split_axis=3, concat_axis=1, tiled=True)  336 us
    all_to_all x2, waiting for transfers between devices, tendency(): lax.all_to_all(by_cols, 'col', split_axis=1, concat_axis=2, tiled=True)  272 us
    another operation x6, other arithmetic, complex_einsum(): return jnp.stack([real_part, imag_part])  119 us
    slice x12, local copies, waits for them, and re-layouts, complex_einsum(): real_part = single(factor[0], values[0]) - single(factor[1], values[1])  79.4 us
    dot_general x8, local copies, waits for them, and re-layouts, single(): jnp.einsum(pattern, factor_part, value_part, precision=lax.Precision.HIGH...  74.2 us
  transfers between devices with their start and end apart: 8, of which 6 were waited for; matrix products, arithmetic and copies ran while one was open for 39% of the time, Pallas kernels for 0%

commit v1 on v0

--- a/solution.py
+++ b/solution.py
@@ -4,6 +4,22 @@
 from jax.sharding import PartitionSpec as P
 
 step_size = 0.25
+
+
+def pairwise_exchange(x, axis, split, join):
+    ways, here = (lax.axis_size(axis), lax.axis_index(axis))
+    width = x.shape[split] // ways
+    dims = list(x.shape)
+    dims[split] = width
+    height = dims[join]
+    dims[join] = height * ways
+    full = jnp.zeros(dims, x.dtype)
+    for mask in range(ways):
+        part = lax.dynamic_slice_in_dim(x, (here ^ mask) * width, width, axis=split)
+        if mask:
+            part = lax.ppermute(part, axis, [(d, d ^ mask) for d in range(ways)])
+        full = lax.dynamic_update_slice_in_dim(full, part, (here ^ mask) * height, axis=join)
+    return full
 
 
 def complex_einsum(pattern, factor, values):
@@ -45,7 +61,7 @@
     lats_row = rows_here // levels
     lats_col = cols_here // levels
     by_rows = block_tile.reshape(2, lats_row, levels, cols_here)
-    regrouped = lax.all_to_all(by_rows, "row", split_axis=3, concat_axis=1, tiled=True)
+    regrouped = pairwise_exchange(by_rows, "row", 3, 1)
     applied = left_apply(regrouped, coupling, vertical, rates)
     left_term = lax.all_to_all(applied, "row", split_axis=1, concat_axis=3, tiled=True)
     left_term = left_term.reshape(2, rows_here, cols_here)

time: 2450 us -> 2200 us (0.90)
  waiting for transfers between devices: 1260 us -> 944 us
  local copies, waits for them, and re-layouts: 457 us -> 495 us
    all_to_all x2 -> x0, waiting for transfers between devices: 336 us -> none  [tendency(): lax.all_to_all(by_rows, 'row', split_axis=3, concat_axis=1, tiled=True)]
    ppermute x0 -> x14, waiting for transfers between devices: none -> 287 us  [pairwise_exchange(): part = lax.ppermute(part, axis, [(d, d ^ mask) for d in range(ways)])]
    all_to_all x2, waiting for transfers between devices: 272 us -> 0.01 us  [tendency(): lax.all_to_all(by_cols, 'col', split_axis=1, concat_axis=2, tiled=True)]
    dynamic_update_slice x0 -> x16, local copies, waits for them, and re-layouts: none -> 46.5 us  [pairwise_exchange(): lax.dynamic_update_slice_in_dim(full, part, (here ^ mask) * height, axis=...]
    unnamed x46 -> x52, local copies, waits for them, and re-layouts: 18.9 us -> 63.4 us
    slice x12 -> x6, local copies, waits for them, and re-layouts: 79.4 us -> 39.4 us  [complex_einsum(): real_part = single(factor[0], values[0]) - single(factor[1], values[1])]
    reshape x2 -> x0, local copies, waits for them, and re-layouts: 35.3 us -> none  [tendency(): by_rows = block_tile.reshape(2, lats_row, levels, cols_here)]
  transfers between devices with their start and end apart: 8 -> 20, of which waited for: 6 -> 8; matrix products, arithmetic and copies ran while one was open for 39% -> 47% of each run, Pallas kernels for 0% -> 0%
where the time goes in v1:
time: 2200 us; the launch traced here: 2180 us
  waiting for transfers between devices  944 us (43%)
  local copies, waits for them, and re-layouts  495 us (22%)
  matrix products  390 us (18%)
  other arithmetic  296 us (13%)
  starting transfers between devices  58.1 us (3%)
    all_to_all x2, waiting for transfers between devices, tendency(): lax.all_to_all(applied_cols, 'col', split_axis=2, concat_axis=1, tiled=True)  657 us
    dot_general x32, matrix products, single(): jnp.einsum(pattern, factor_part, value_part, precision=lax.Precision.HIGH...  390 us
    ppermute x14, waiting for transfers between devices, pairwise_exchange(): part = lax.ppermute(part, axis, [(d, d ^ mask) for d in range(ways)])  287 us
    another operation x6, other arithmetic, complex_einsum(): return jnp.stack([real_part, imag_part])  119 us
    dot_general x8, local copies, waits for them, and re-layouts, single(): jnp.einsum(pattern, factor_part, value_part, precision=lax.Precision.HIGH...  74.6 us
    unnamed x52, local copies, waits for them, and re-layouts  63.4 us
    sub x4, other arithmetic, complex_scale(): real_part = factor[0] * values[0] - factor[1] * values[1]  52 us
    dynamic_update_slice x16, local copies, waits for them, and re-layouts, pairwise_exchange(): lax.dynamic_update_slice_in_dim(full, part, (here ^ mask) * height, axis=...  46.5 us
  transfers between devices with their start and end apart: 20, of which 8 were waited for; matrix products, arithmetic and copies ran while one was open for 47% of the time, Pallas kernels for 0%

profile of v1, /device:TPU:0, one launch (start us, length us, event | category | flops | bytes accessed | tf_op | source)
XLA Modules:
  0.0 2184.3 jit_solution(3030562245335714981)
XLA Ops:
  63.0 27.8 %collective-permute-done.1 = f32[2,8,128,256]{2,3,1,0:T(8,128)} collective-permute-done((f32[2,8,128,256]{2,3,1,0:T(8,128)}, f32[2,8,128,256]{2,3,1,0:T(8,128)}, u32[]{:S(2)}, u32[]{:S(2)}) %collective-permute-start.1) | collective-permute-done | bytes 2097184 | tf_op jit(solution)/shard_map/ppermute | solution.py:20
  110.4 24.9 %collective-permute-done.2 = f32[2,8,128,256]{2,3,1,0:T(8,128)} collective-permute-done((f32[2,8,128,256]{2,3,1,0:T(8,128)}, f32[2,8,128,256]{2,3,1,0:T(8,128)}, u32[]{:S(2)}, u32[]{:S(2)}) %collective-permute-start.2) | collective-permute-done | bytes 2097184 | tf_op jit(solution)/shard_map/ppermute | solution.py:20
  141.6 90.7 %collective-permute-done.4 = f32[2,8,128,256]{2,3,1,0:T(8,128)} collective-permute-done((f32[2,8,128,256]{2,3,1,0:T(8,128)}, f32[2,8,128,256]{2,3,1,0:T(8,128)}, u32[]{:S(2)}, u32[]{:S(2)}) %collective-permute-start.4) | collective-permute-done | bytes 2097184 | tf_op jit(solution)/shard_map/ppermute | solution.py:20
  403.3 19.0 add_bitcast_fusion.4
  527.7 17.4 fusion.22
  589.3 41.0 %fusion.6 = (f32[1,256,64,128]{3,1,2,0:T(8,128)}, f32[1,256,64,128]{3,1,2,0:T(8,128)}) fusion(f32[256,128,64]{1,2,0:T(8,128)} %fusion.20, f32[256,128,64]{1,2,0:T(8,128)} %fusion.16, f32[256,128,64]{1,2,0:T(8,128)} %fusion.18, f32[256,128,64]{1,2,0:T(8,128)} %fusion.22), kind=kLoop, calls=%fused_computation.16 | loop fusion | flops 4194304 | bytes 50331648 | tf_op jit(solution)/shard_map/stack | solution.py:32
  660.1 17.4 copy.120
  677.5 18.0 reshape.151
  695.5 328.6 %all-to-all-done.2 = f32[2,256,64,128]{3,1,0,2:T(8,128)} async-done(((f32[2,256,64,128]{3,1,0,2:T(8,128)}), f32[2,256,64,128]{3,1,0,2:T(8,128)}, u32[]{:S(2)}, u32[]{:S(2)}) %all-to-all-start.2) | async-done | bytes 16777248 | tf_op jit(solution)/shard_map/all_to_all | solution.py:71
  1024.1 17.8 copy.223
  1041.8 18.0 reshape.153
  1059.8 29.2 %multiply_add_fusion.1 = f32[2,1024,2048]{2,1,0:T(8,128)} fusion(f32[2,1024,2048]{2,1,0:T(8,128)} %param.6, f32[2,1024,2048]{2,1,0:T(8,128)} %param.7, f32[2,1024,2048]{2,1,0:T(8,128)} %reshape.151, f32[2,1024,2048]{2,1,0:T(8,128)} %reshape.153), kind=kLoop, calls=%fused_computation.10 | loop fusion | flops 16777216 | bytes 83886080 | tf_op jit(solution)/shard_map/add | solution.py:80
  1151.4 27.8 %collective-permute-done.8 = f32[2,8,128,256]{2,3,1,0:T(8,128)} collective-permute-done((f32[2,8,128,256]{2,3,1,0:T(8,128)}, f32[2,8,128,256]{2,3,1,0:T(8,128)}, u32[]{:S(2)}, u32[]{:S(2)}) %collective-permute-start.8) | collective-permute-done | bytes 2097184 | tf_op jit(solution)/shard_map/ppermute | solution.py:20
  1198.6 25.1 %collective-permute-done.9 = f32[2,8,128,256]{2,3,1,0:T(8,128)} collective-permute-done((f32[2,8,128,256]{2,3,1,0:T(8,128)}, f32[2,8,128,256]{2,3,1,0:T(8,128)}, u32[]{:S(2)}, u32[]{:S(2)}) %collective-permute-start.9) | collective-permute-done | bytes 2097184 | tf_op jit(solution)/shard_map/ppermute | solution.py:20
  1229.9 90.4 %collective-permute-done.11 = f32[2,8,128,256]{2,3,1,0:T(8,128)} collective-permute-done((f32[2,8,128,256]{2,3,1,0:T(8,128)}, f32[2,8,128,256]{2,3,1,0:T(8,128)}, u32[]{:S(2)}, u32[]{:S(2)}) %collective-permute-start.11) | collective-permute-done | bytes 2097184 | tf_op jit(solution)/shard_map/ppermute | solution.py:20
  1570.8 17.4 fusion.14
  1677.2 18.2 fusion.5
  1695.4 18.4 fusion.4
  1754.9 17.4 copy.154
  1772.3 18.0 reshape.155
  1790.3 328.6 %all-to-all-done.5 = f32[2,256,64,128]{3,1,0,2:T(8,128)} async-done(((f32[2,256,64,128]{3,1,0,2:T(8,128)}), f32[2,256,64,128]{3,1,0,2:T(8,128)}, u32[]{:S(2)}, u32[]{:S(2)}) %all-to-all-start.5) | async-done | bytes 16777248 | tf_op jit(solution)/shard_map/all_to_all | solution.py:71
  2118.9 17.8 copy.170
  2136.7 18.0 reshape.157
  2154.7 29.2 %multiply_add_fusion = f32[2,1024,2048]{2,1,0:T(8,128)} fusion(f32[2,1024,2048]{2,1,0:T(8,128)} %param.6, f32[2,1024,2048]{2,1,0:T(8,128)} %param.7, f32[2,1024,2048]{2,1,0:T(8,128)} %reshape.155, f32[2,1024,2048]{2,1,0:T(8,128)} %reshape.157), kind=kLoop, calls=%fused_computation.9 | loop fusion | flops 16777216 | bytes 83886080 | tf_op jit(solution)/shard_map/add | solution.py:81
  (172 shorter events, 907.4 us)
Async XLA Ops:
  16.5 428.8 %all-to-all-start.1 = ((f32[2,1024,16,128]{3,2,0,1:T(8,128)}), f32[2,1024,16,128]{3,2,0,1:T(8,128)}, u32[]{:S(2)}, u32[]{:S(2)}) async-start(f32[2,1024,16,128]{3,2,0,1:T(8,128)} %copy.171), calls=%async_computation.1 | async-start | bytes 33554432 | tf_op jit(solution)/shard_map/all_to_all | solution.py:69
  38.0 19.4 collective-permute-start
  41.5 49.3 %collective-permute-start.1 = (f32[2,8,128,256]{2,3,1,0:T(8,128)}, f32[2,8,128,256]{2,3,1,0:T(8,128)}, u32[]{:S(2)}, u32[]{:S(2)}) collective-permute-start(f32[2,8,128,256]{2,3,1,0:T(8,128)} %copy.174), channel_id=1, source_target_pairs={{0,8},{4,12},{8,0},{12,4},{16,24},{20,28},{24,16},{28,20},{1,9},{5... | collective-permute-start | bytes 6291464 | tf_op jit(solution)/shard_map/ppermute | solution.py:20
  46.9 88.5 %collective-permute-start.2 = (f32[2,8,128,256]{2,3,1,0:T(8,128)}, f32[2,8,128,256]{2,3,1,0:T(8,128)}, u32[]{:S(2)}, u32[]{:S(2)}) collective-permute-start(f32[2,8,128,256]{2,3,1,0:T(8,128)} %copy.175), channel_id=1, source_target_pairs={{0,12},{4,8},{8,4},{12,0},{16,28},{20,24},{24,20},{28,16},{1,13},{... | collective-permute-start | bytes 6291464 | tf_op jit(solution)/shard_map/ppermute | solution.py:20
  49.9 88.5 %collective-permute-start.3 = (f32[2,8,128,256]{2,3,1,0:T(8,128)}, f32[2,8,128,256]{2,3,1,0:T(8,128)}, u32[]{:S(2)}, u32[]{:S(2)}) collective-permute-start(f32[2,8,128,256]{2,3,1,0:T(8,128)} %copy.176), channel_id=1, source_target_pairs={{0,16},{4,20},{8,24},{12,28},{16,0},{20,4},{24,8},{28,12},{1,17},{... | collective-permute-start | bytes 6291464 | tf_op jit(solution)/shard_map/ppermute | solution.py:20
  54.6 177.6 %collective-permute-start.4 = (f32[2,8,128,256]{2,3,1,0:T(8,128)}, f32[2,8,128,256]{2,3,1,0:T(8,128)}, u32[]{:S(2)}, u32[]{:S(2)}) collective-permute-start(f32[2,8,128,256]{2,3,1,0:T(8,128)} %copy.177), channel_id=1, source_target_pairs={{0,20},{4,16},{8,28},{12,24},{16,4},{20,0},{24,12},{28,8},{1,21},{... | collective-permute-start | bytes 6291464 | tf_op jit(solution)/shard_map/ppermute | solution.py:20
  57.5 177.8 %collective-permute-start.5 = (f32[2,8,128,256]{2,3,1,0:T(8,128)}, f32[2,8,128,256]{2,3,1,0:T(8,128)}, u32[]{:S(2)}, u32[]{:S(2)}) collective-permute-start(f32[2,8,128,256]{2,3,1,0:T(8,128)} %copy.178), channel_id=1, source_target_pairs={{0,24},{4,28},{8,16},{12,20},{16,8},{20,12},{24,0},{28,4},{1,25},{... | collective-permute-start | bytes 6291464 | tf_op jit(solution)/shard_map/ppermute | solution.py:20
  90.7 147.7 %collective-permute-start.6 = (f32[2,8,128,256]{2,3,1,0:T(8,128)}, f32[2,8,128,256]{2,3,1,0:T(8,128)}, u32[]{:S(2)}, u32[]{:S(2)}) collective-permute-start(f32[2,8,128,256]{2,3,1,0:T(8,128)} %copy.179), channel_id=1, source_target_pairs={{0,28},{4,24},{8,20},{12,16},{16,12},{20,8},{24,4},{28,0},{1,29},{... | collective-permute-start | bytes 6291464 | tf_op jit(solution)/shard_map/ppermute | solution.py:20
  94.4 147.2 %copy-start.8 = (f32[64,128]{1,0:T(8,128)}, f32[64,128]{1,0:T(8,128)S(1)}, u32[]{:S(2)}) copy-start(f32[64,128]{1,0:T(8,128)S(1)} %neg.27) | copy-start | bytes 98308
  138.4 103.1 %copy-start.12 = (f32[64,128]{1,0:T(8,128)S(1)}, f32[64,128]{1,0:T(8,128)}, u32[]{:S(2)}) copy-start(f32[64,128]{1,0:T(8,128)} %param.11) | copy-start | bytes 98308
  445.2 207.8 %all-to-all-start = ((f32[2,64,128,256]{2,3,0,1:T(8,128)}), f32[2,64,128,256]{2,3,0,1:T(8,128)}, u32[]{:S(2)}, u32[]{:S(2)}) async-start(f32[2,64,128,256]{2,3,0,1:T(8,128)} %copy.119), calls=%async_computation | async-start | bytes 33554432 | tf_op jit(solution)/shard_map/all_to_all | solution.py:66
  451.5 130.8 %copy-start.14 = (f32[64,128]{1,0:T(8,128)}, f32[64,128]{1,0:T(8,128)S(1)}, u32[]{:S(2)}) copy-start(f32[64,128]{1,0:T(8,128)S(1)} %neg.32) | copy-start | bytes 98308
  653.1 371.0 %all-to-all-start.2 = ((f32[2,256,64,128]{3,1,0,2:T(8,128)}), f32[2,256,64,128]{3,1,0,2:T(8,128)}, u32[]{:S(2)}, u32[]{:S(2)}) async-start(f32[2,256,64,128]{3,1,0,2:T(8,128)} %copy.135), calls=%async_computation.2 | async-start | bytes 33554432 | tf_op jit(solution)/shard_map/all_to_all | solution.py:71
  1105.5 431.5 %all-to-all-start.4 = ((f32[2,1024,16,128]{3,2,0,1:T(8,128)}), f32[2,1024,16,128]{3,2,0,1:T(8,128)}, u32[]{:S(2)}, u32[]{:S(2)}) async-start(f32[2,1024,16,128]{3,2,0,1:T(8,128)} %copy.155), calls=%async_computation.4 | async-start | bytes 33554432 | tf_op jit(solution)/shard_map/all_to_all | solution.py:69
  1127.1 18.6 collective-permute-start.7
  1130.1 49.0 %collective-permute-start.8 = (f32[2,8,128,256]{2,3,1,0:T(8,128)}, f32[2,8,128,256]{2,3,1,0:T(8,128)}, u32[]{:S(2)}, u32[]{:S(2)}) collective-permute-start(f32[2,8,128,256]{2,3,1,0:T(8,128)} %copy.182), channel_id=1, source_target_pairs={{0,8},{4,12},{8,0},{12,4},{16,24},{20,28},{24,16},{28,20},{1,9},{5... | collective-permute-start | bytes 6291464 | tf_op jit(solution)/shard_map/ppermute | solution.py:20
  1135.3 88.4 %collective-permute-start.9 = (f32[2,8,128,256]{2,3,1,0:T(8,128)}, f32[2,8,128,256]{2,3,1,0:T(8,128)}, u32[]{:S(2)}, u32[]{:S(2)}) collective-permute-start(f32[2,8,128,256]{2,3,1,0:T(8,128)} %copy.183), channel_id=1, source_target_pairs={{0,12},{4,8},{8,4},{12,0},{16,28},{20,24},{24,20},{28,16},{1,13},{... | collective-permute-start | bytes 6291464 | tf_op jit(solution)/shard_map/ppermute | solution.py:20
  1138.2 88.6 %collective-permute-start.10 = (f32[2,8,128,256]{2,3,1,0:T(8,128)}, f32[2,8,128,256]{2,3,1,0:T(8,128)}, u32[]{:S(2)}, u32[]{:S(2)}) collective-permute-start(f32[2,8,128,256]{2,3,1,0:T(8,128)} %copy.184), channel_id=1, source_target_pairs={{0,16},{4,20},{8,24},{12,28},{16,0},{20,4},{24,8},{28,12},{1,17},{... | collective-permute-start | bytes 6291464 | tf_op jit(solution)/shard_map/ppermute | solution.py:20
  1142.8 177.6 %collective-permute-start.11 = (f32[2,8,128,256]{2,3,1,0:T(8,128)}, f32[2,8,128,256]{2,3,1,0:T(8,128)}, u32[]{:S(2)}, u32[]{:S(2)}) collective-permute-start(f32[2,8,128,256]{2,3,1,0:T(8,128)} %copy.185), channel_id=1, source_target_pairs={{0,20},{4,16},{8,28},{12,24},{16,4},{20,0},{24,12},{28,8},{1,21},{... | collective-permute-start | bytes 6291464 | tf_op jit(solution)/shard_map/ppermute | solution.py:20
  1145.7 177.7 %collective-permute-start.12 = (f32[2,8,128,256]{2,3,1,0:T(8,128)}, f32[2,8,128,256]{2,3,1,0:T(8,128)}, u32[]{:S(2)}, u32[]{:S(2)}) collective-permute-start(f32[2,8,128,256]{2,3,1,0:T(8,128)} %copy.186), channel_id=1, source_target_pairs={{0,24},{4,28},{8,16},{12,20},{16,8},{20,12},{24,0},{28,4},{1,25},{... | collective-permute-start | bytes 6291464 | tf_op jit(solution)/shard_map/ppermute | solution.py:20
  1179.2 147.4 %collective-permute-start.13 = (f32[2,8,128,256]{2,3,1,0:T(8,128)}, f32[2,8,128,256]{2,3,1,0:T(8,128)}, u32[]{:S(2)}, u32[]{:S(2)}) collective-permute-start(f32[2,8,128,256]{2,3,1,0:T(8,128)} %copy.187), channel_id=1, source_target_pairs={{0,28},{4,24},{8,20},{12,16},{16,12},{20,8},{24,4},{28,0},{1,29},{... | collective-permute-start | bytes 6291464 | tf_op jit(solution)/shard_map/ppermute | solution.py:20
  1537.0 210.7 %all-to-all-start.3 = ((f32[2,64,128,256]{2,3,0,1:T(8,128)}), f32[2,64,128,256]{2,3,0,1:T(8,128)}, u32[]{:S(2)}, u32[]{:S(2)}) async-start(f32[2,64,128,256]{2,3,0,1:T(8,128)} %copy.153), calls=%async_computation.3 | async-start | bytes 33554432 | tf_op jit(solution)/shard_map/all_to_all | solution.py:66
  1561.8 106.1 %copy-start = (f32[1,256,4,16,128]{4,1,3,2,0:T(8,128)}, f32[1,256,4,16,128]{4,1,3,2,0:T(8,128)S(1)}, u32[]{:S(2)}) copy-start(f32[1,256,4,16,128]{4,1,3,2,0:T(8,128)S(1)} %copy.157) | copy-start | bytes 25165828
  1747.6 371.3 %all-to-all-start.5 = ((f32[2,256,64,128]{3,1,0,2:T(8,128)}), f32[2,256,64,128]{3,1,0,2:T(8,128)}, u32[]{:S(2)}, u32[]{:S(2)}) async-start(f32[2,256,64,128]{3,1,0,2:T(8,128)} %copy.169), calls=%async_computation.5 | async-start | bytes 33554432 | tf_op jit(solution)/shard_map/all_to_all | solution.py:71
  (13 other events, 434.4 us)
